TPU v7x, 32 devices: a whole 2x2x4 slice. The times are simulated.
32 devices in a mesh: mode: 8 (over y, x, core), orb: 4 (over z).
Axes of the slice: x: 2, y: 2, z: 4, core: 2. Of those that a mesh axis runs over, the one named last changes fastest.
Arguments:
- correlators: float32 [512, 2, 256, 256], P('mode', None, 'orb'), may hold values from -6 to 6
- density: float32 [2, 256, 256], P(None, 'orb'), may hold values from -6 to 6
- bare_hamiltonian: float32 [2, 256, 256], P(None, 'orb'), may hold values from -0.375 to 0.375
- coupling: float32 [512], P('mode'), may hold values from -0.25 to 0.25
- propagator: float32 [512, 512], P('mode'), may hold values from -0.25 to 0.25
Outputs:
- correlators_out: float32 [512, 2, 256, 256], P('mode', None, 'orb')
- density_out: float32 [2, 256, 256], P(None, 'orb')
All inputs are finite; a program needn't handle non-finite values.
Results may differ from a plain program's by a relative error of at most 0.0001.
Values sent between devices are 32-bit elements; how exact they have to be, the bound alone decides.
No kernel may reach another device: no remote copies, remote signals or barrier semaphores. Data moves between devices by JAX's collectives and lax.ppermute only.
A program may use at most 128 MiB of HBM per device.

v0:
```python
import jax
import jax.numpy as jnp
from jax import lax
from jax.sharding import PartitionSpec as P

time_step = 0.1
field_weight = 0.0625


def contract(form, first, second):
    return jnp.einsum(form, first, second, precision=lax.Precision.HIGHEST)


def left_product(matrix, stack):
    real = contract("ij,mjk->mik", matrix[0], stack[:, 0]) - contract(
        "ij,mjk->mik", matrix[1], stack[:, 1]
    )
    imag = contract("ij,mjk->mik", matrix[0], stack[:, 1]) + contract(
        "ij,mjk->mik", matrix[1], stack[:, 0]
    )
    return jnp.stack([real, imag], axis=1)


def right_product(stack, matrix):
    real = contract("mij,jk->mik", stack[:, 0], matrix[0]) - contract(
        "mij,jk->mik", stack[:, 1], matrix[1]
    )
    imag = contract("mij,jk->mik", stack[:, 0], matrix[1]) + contract(
        "mij,jk->mik", stack[:, 1], matrix[0]
    )
    return jnp.stack([real, imag], axis=1)


def advance(stack, commut, weights, dens):
    turned = jnp.stack([commut[:, 1], -commut[:, 0]], axis=1)
    return stack + time_step * turned + time_step * weights[:, None, None, None] * dens[None]


def modes_substep(stacks, dens, hamil, bare_full, weights):
    commut = left_product(hamil, stacks) - right_product(stacks, hamil)
    updated = advance(stacks, commut, weights, dens)
    partial_value = contract("m,mcij->cij", weights, updated)
    collision = lax.psum(partial_value, ("mode", "orb"))
    dens = dens + time_step * collision
    return (updated, dens, bare_full + field_weight * dens)


def to_whole(stacks):
    return lax.all_to_all(stacks, "orb", split_axis=0, concat_axis=2, tiled=True)


def to_split(stacks):
    return lax.all_to_all(stacks, "orb", split_axis=2, concat_axis=0, tiled=True)


def propagate(stacks, propagator):
    local_modes = stacks.shape[0]
    groups = lax.axis_size("mode")
    flat = stacks.reshape(local_modes, groups, -1)
    spread = lax.all_to_all(flat, "mode", split_axis=1, concat_axis=0, tiled=True)
    entries = spread[:, 0, :]
    mixed = contract("mn,nx->mx", lax.all_gather(propagator, "mode", axis=0, tiled=True), entries)
    returned = lax.all_to_all(mixed[:, None, :], "mode", split_axis=0, concat_axis=1, tiled=True)
    return returned.reshape(stacks.shape)


def on_device(correlators, density, bare_hamiltonian, coupling, propagator):
    dens, bare_full = (
        lax.all_gather(density, "orb", axis=1, tiled=True),
        lax.all_gather(bare_hamiltonian, "orb", axis=1, tiled=True),
    )
    hamil = bare_full + field_weight * dens
    owned = correlators.shape[0] // lax.axis_size("orb")
    weights = lax.dynamic_slice_in_dim(coupling, lax.axis_index("orb") * owned, owned, 0)
    whole = to_whole(correlators)
    for turn in range(2):
        whole, dens, hamil = modes_substep(whole, dens, hamil, bare_full, weights)
    stacks = propagate(to_split(whole), propagator)
    whole = to_whole(stacks)
    whole, dens, hamil = modes_substep(whole, dens, hamil, bare_full, weights)
    stacks = to_split(whole)
    row_count = density.shape[1]
    dens_rows = lax.dynamic_slice_in_dim(dens, lax.axis_index("orb") * row_count, row_count, 1)
    return (stacks, dens_rows)


def solution(mesh):
    in_specs = (
        P("mode", None, "orb", None),
        P(None, "orb", None),
        P(None, "orb", None),
        P("mode"),
        P("mode", None),
    )
    out_specs = (P("mode", None, "orb", None), P(None, "orb", None))
    return jax.shard_map(
        on_device, mesh=mesh, in_specs=in_specs, out_specs=out_specs, check_vma=False
    )
```

profile of v0, /device:TPU:0, one launch (start us, length us, event | category | flops | bytes accessed | tf_op | source)
XLA Modules:
  0.0 1640.5 jit_solution(9633585185455088017)
XLA Ops:
  14.6 194.0 %all_gather.10 = f32[2,256,256]{2,1,0:T(8,128)S(1)} all-gather(f32[2,64,256]{2,1,0:T(8,128)S(1)} %copy-done.12), channel_id=1, replica_groups=mesh['mode'=8,'orb'=4] {'orb'}, dimensions={1}, use_global_device_ids=true | all-gather | bytes 655360 | tf_op jit(solution)/shard_map/all_gather | solution.py:69
  208.6 15.9 all_gather.9
  250.7 13.2 subtract_bitcast_fusion.5
  282.9 7.8 fusion.10
  291.5 130.2 %all-reduce.4.cloned.1.call-done = f32[2,256,256]{2,1,0:T(8,128)} async-done(((f32[2,256,256]{2,1,0:T(8,128)}), f32[2,256,256]{2,1,0:T(8,128)}) %all-reduce.4.cloned.1.call-update) | async-done | bytes 524304 | tf_op jit(solution)/shard_map/psum | solution.py:43
  477.2 8.3 copy.81
  485.4 186.8 %all_to_all.99 = f32[16,2,256,256]{3,0,1,2:T(8,128)S(1)} all-to-all(f32[16,2,256,256]{3,0,1,2:T(8,128)} %copy.81), channel_id=1, replica_groups=mesh['mode'=8,'orb'=4] {'orb'}, dimensions={2} | all-to-all | bytes 16777216 | tf_op jit(solution)/shard_map/all_to_all | solution.py:53
  672.3 8.3 copy.145
  680.5 9.4 reshape.18
  689.9 11.6 copy.83
  707.1 56.9 %all-gather.2.cloned.1.call-done = f32[512,512]{1,0:T(8,128)} async-done(((f32[64,512]{1,0:T(8,128)}), f32[512,512]{1,0:T(8,128)}) %all-gather.2.cloned.1.call-update) | async-done | bytes 1048592 | tf_op jit(solution)/shard_map/all_gather | solution.py:62
  764.0 40.7 %all-to-all-done.2 = f32[64,8,4096]{2,0,1:T(8,128)} async-done(((f32[64,8,4096]{2,0,1:T(8,128)}), f32[64,8,4096]{2,0,1:T(8,128)}, u32[]{:S(2)}, u32[]{:S(2)}) %all-to-all-start.2) | async-done | bytes 8388640 | tf_op jit(solution)/shard_map/all_to_all | solution.py:60
  804.7 30.3 %convolution_bitcast_fusion = f32[512,1,4096]{0,2,1:T(8,128)} fusion(f32[512,4096]{1,0:T(8,128)} %bitcast.41, f32[512,512]{1,0:T(8,128)} %all-gather.2.cloned.1.call-done), kind=kOutput, calls=%fused_computation.19 | convolution fusion | flops 12884901888 | bytes 17825792 | tf_op jit(solution)/shard_map/mn,nx->mx/dot_general | solution.py:11
  835.0 19.3 %copy.84 = f32[512,1,4096]{2,1,0:T(1,128)} copy(f32[512,1,4096]{0,2,1:T(8,128)} %convolution_bitcast_fusion) | data formatting | bytes 16777216 | tf_op jit(solution)/shard_map/broadcast_in_dim | solution.py:63
  854.3 97.8 %all_to_all.100 = f32[512,1,4096]{2,1,0:T(1,128)S(1)} all-to-all(f32[512,1,4096]{2,1,0:T(1,128)} %copy.84), channel_id=1, replica_groups=mesh['mode'=8,'orb'=4] {'mode'}, dimensions={0} | all-to-all | bytes 16777216 | tf_op jit(solution)/shard_map/all_to_all | solution.py:63
  952.1 8.1 copy.134
  960.2 8.5 copy.85
  968.6 9.4 reshape.19
  983.8 12.9 fusion.8
  997.5 272.8 %all-reduce.6.cloned.1.call-done = f32[2,256,256]{2,1,0:T(8,128)} async-done(((f32[2,256,256]{2,1,0:T(8,128)}), f32[2,256,256]{2,1,0:T(8,128)}) %all-reduce.6.cloned.1.call-update) | async-done | bytes 524304 | tf_op jit(solution)/shard_map/psum | solution.py:43
  1319.6 8.3 copy.95
  1333.6 12.7 fusion.6
  1347.1 272.6 %all-reduce.8.cloned.1.call-done = f32[2,256,256]{2,1,0:T(8,128)} async-done(((f32[2,256,256]{2,1,0:T(8,128)}), f32[2,256,256]{2,1,0:T(8,128)}) %all-reduce.8.cloned.1.call-update) | async-done | bytes 524304 | tf_op jit(solution)/shard_map/psum | solution.py:43
  1621.3 11.6 copy.96
  (92 shorter events, 177.3 us)
Async XLA Ops:
  8.0 6.5 copy-start.14
  8.0 6.6 copy-start.12
  8.0 200.5 %copy-start.13 = (f32[2,64,256]{2,1,0:T(8,128)S(1)}, f32[2,64,256]{2,1,0:T(8,128)}, u32[]{:S(2)}) copy-start(f32[2,64,256]{2,1,0:T(8,128)} %param.7) | copy-start | bytes 393220
  8.0 216.6 %all-to-all-start = ((f32[64,2,64,256]{3,2,1,0:T(8,128)}), f32[64,2,64,256]{3,2,1,0:T(8,128)}, u32[]{:S(2)}, u32[]{:S(2)}) async-start(f32[64,2,64,256]{3,2,1,0:T(8,128)} %param.5), calls=%async_computation | async-start | bytes 16777216 | tf_op jit(solution)/shard_map/all_to_all | solution.py:49
  14.5 407.2 %all-reduce.4.cloned.1.call-start = ((), (), s32[]{:S(2)}) async-start(), calls=%async_computation.6 | async-start | bytes 1048576 | tf_op jit(solution)/shard_map/psum | solution.py:43
  208.6 213.2 %copy-start.8 = (f32[2,256,256]{2,1,0:T(8,128)}, f32[2,256,256]{2,1,0:T(8,128)S(1)}, u32[]{:S(2)}) copy-start(f32[2,256,256]{2,1,0:T(8,128)S(1)} %all_gather.10) | copy-start | bytes 1572868
  224.5 197.2 %copy-start.9 = (f32[2,256,256]{2,1,0:T(8,128)}, f32[2,256,256]{2,1,0:T(8,128)S(1)}, u32[]{:S(2)}) copy-start(f32[2,256,256]{2,1,0:T(8,128)S(1)} %all_gather.9) | copy-start | bytes 1572868
  228.7 45.9 %copy-start = (f32[4,16,2,64,256]{4,3,0,1,2:T(8,128)}, f32[4,16,2,64,256]{4,3,0,1,2:T(8,128)S(1)}, u32[]{:S(2)}) copy-start(f32[4,16,2,64,256]{4,3,0,1,2:T(8,128)S(1)} %copy.64) | copy-start | bytes 25165828
  274.6 4.9 copy-start.5
  279.5 3.4 copy-start.1
  421.7 8.2 copy-start.2
  456.3 5.4 copy-start.7
  456.3 14.0 slice-start
  461.7 8.6 slice-start.1
  466.0 4.3 copy-start.6
  477.2 8.3 copy-start.3
  701.5 103.2 %all-to-all-start.2 = ((f32[64,8,4096]{2,0,1:T(8,128)}), f32[64,8,4096]{2,0,1:T(8,128)}, u32[]{:S(2)}, u32[]{:S(2)}) async-start(f32[64,8,4096]{2,0,1:T(8,128)} %copy.83), calls=%async_computation.2 | async-start | bytes 16777216 | tf_op jit(solution)/shard_map/all_to_all | solution.py:60
  706.5 57.5 %all-gather.2.cloned.1.call-start = ((), (), s32[]{:S(2)}) async-start(), calls=%async_computation.7 | async-start | bytes 1179648 | tf_op jit(solution)/shard_map/all_gather | solution.py:62
  978.0 293.5 %all-to-all-start.4 = ((f32[64,2,64,256]{3,2,1,0:T(8,128)}), f32[64,2,64,256]{3,2,1,0:T(8,128)}, u32[]{:S(2)}, u32[]{:S(2)}) async-start(f32[64,2,64,256]{3,2,1,0:T(8,128)} %reshape.19), calls=%async_computation.4 | async-start | bytes 16777216 | tf_op jit(solution)/shard_map/all_to_all | solution.py:49
  983.7 286.7 %copy-start.10 = (f32[2,256,256]{2,1,0:T(8,128)S(1)}, f32[2,256,256]{2,1,0:T(8,128)}, u32[]{:S(2)}) copy-start(f32[2,256,256]{2,1,0:T(8,128)} %copy-done.9) | copy-start | bytes 1572868
  983.7 286.7 %copy-start.11 = (f32[2,256,256]{2,1,0:T(8,128)S(1)}, f32[2,256,256]{2,1,0:T(8,128)}, u32[]{:S(2)}) copy-start(f32[2,256,256]{2,1,0:T(8,128)} %get-tuple-element.5) | copy-start | bytes 1572868
  983.7 286.7 %all-reduce.6.cloned.1.call-start = ((), (), s32[]{:S(2)}) async-start(), calls=%async_computation.8 | async-start | bytes 1048576 | tf_op jit(solution)/shard_map/psum | solution.py:43
  1327.9 293.5 %all-to-all-start.5 = ((f32[16,2,256,256]{3,0,1,2:T(8,128)}), f32[16,2,256,256]{3,0,1,2:T(8,128)}, u32[]{:S(2)}, u32[]{:S(2)}) async-start(f32[16,2,256,256]{3,0,1,2:T(8,128)} %copy.95), calls=%async_computation.5 | async-start | bytes 16777216 | tf_op jit(solution)/shard_map/all_to_all | solution.py:53
  1333.5 286.2 %all-reduce.8.cloned.1.call-start = ((), (), s32[]{:S(2)}) async-start(), calls=%async_computation.9 | async-start | bytes 1048576 | tf_op jit(solution)/shard_map/psum | solution.py:43
  (1 other events, 3.3 us)
Sparse Core Ops, SparseCore 0:
  291.7 130.0 all-reduce.3
  997.6 272.6 all-reduce.5
  1347.2 272.4 all-reduce.7
Sparse Core Ops, SparseCore 1:
  708.9 55.1 all-gather.1
where the time goes:
time: 1650 us; the launch traced here: 1640 us
  waiting for transfers between devices  774 us (47%)
  blocking collectives  494 us (30%)
  matrix products  174 us (11%)
  local copies, waits for them, and re-layouts  120 us (7%)
  other arithmetic  39.6 us (2%)
  starting transfers between devices  22.9 us (1%)
    psum x3, waiting for transfers between devices, modes_substep(): collision = lax.psum(partial_value, ('mode', 'orb'))  676 us
    all_gather x1, blocking collectives, on_device(): lax.all_gather(density, 'orb', axis=1, tiled=True)  194 us
    all_to_all x1, blocking collectives, to_split(): lax.all_to_all(stacks, 'orb', split_axis=2, concat_axis=0, tiled=True)  187 us
    dot_general x28, matrix products, contract(): return jnp.einsum(form, first, second, precision=lax.Precision.HIGHEST)  174 us
    all_to_all x1, blocking collectives, propagate(): lax.all_to_all(mixed[:, None, :], 'mode', split_axis=0, concat_axis=1, ti...  97.8 us
    all_gather x1, waiting for transfers between devices, propagate(): lax.all_gather(propagator, 'mode', axis=0, tiled=True)  56.9 us
    all_to_all x1, waiting for transfers between devices, propagate(): lax.all_to_all(flat, 'mode', split_axis=1, concat_axis=0, tiled=True)  40.7 us
  transfers between devices with their start and end apart: 8, of which 5 were waited for; matrix products, arithmetic and copies ran while one was open for 2% of the time, Pallas kernels for 0%

commit v1 on v0

--- a/solution.py
+++ b/solution.py
@@ -40,7 +40,7 @@
     commut = left_product(hamil, stacks) - right_product(stacks, hamil)
     updated = advance(stacks, commut, weights, dens)
     partial_value = contract("m,mcij->cij", weights, updated)
-    collision = lax.psum(partial_value, ("mode", "orb"))
+    collision = jnp.sum(lax.all_gather(partial_value, ("mode", "orb")), axis=0)
     dens = dens + time_step * collision
     return (updated, dens, bare_full + field_weight * dens)
 

time: 1650 us -> 1610 us (0.976)
  blocking collectives: 494 us -> 308 us
  waiting for transfers between devices: 774 us -> 884 us
  other arithmetic: 39.6 us -> 57.1 us
    psum x3 -> x0, waiting for transfers between devices: 676 us -> none  [modes_substep(): collision = lax.psum(partial_value, ('mode', 'orb'))]
    all_to_all x1 -> x2, waiting for transfers between devices: 0.01 us -> 498 us  [to_split(): lax.all_to_all(stacks, 'orb', split_axis=2, concat_axis=0, tiled=True)]
    all_to_all x1 -> x0, blocking collectives: 187 us -> none  [to_split(): lax.all_to_all(stacks, 'orb', split_axis=2, concat_axis=0, tiled=True)]
    all_to_all x2, waiting for transfers between devices: 0.01 us -> 176 us  [to_whole(): lax.all_to_all(stacks, 'orb', split_axis=0, concat_axis=2, tiled=True)]
    all_gather x0 -> x3, waiting for transfers between devices: none -> 116 us  [modes_substep(): collision = jnp.sum(lax.all_gather(partial_value, ('mode', 'orb')), axis=0)]
    all_gather x1, waiting for transfers between devices: 56.9 us -> 0.03 us  [propagate(): lax.all_gather(propagator, 'mode', axis=0, tiled=True)]
    all_to_all x1, waiting for transfers between devices: 40.7 us -> 94 us  [propagate(): lax.all_to_all(flat, 'mode', split_axis=1, concat_axis=0, tiled=True)]
    reduce_sum x0 -> x3, other arithmetic: none -> 20.8 us  [modes_substep(): collision = jnp.sum(lax.all_gather(partial_value, ('mode', 'orb')), axis=0)]
  transfers between devices with their start and end apart: 8 -> 9, of which waited for: 5 -> 5; matrix products, arithmetic and copies ran while one was open for 2% -> 10% of each run, Pallas kernels for 0% -> 0%
where the time goes in v1:
time: 1610 us; the launch traced here: 1590 us
  waiting for transfers between devices  884 us (55%)
  blocking collectives  308 us (19%)
  matrix products  170 us (11%)
  local copies, waits for them, and re-layouts  131 us (8%)
  other arithmetic  57.1 us (4%)
  starting transfers between devices  28.5 us (2%)
  between operations  16.4 us (1%)
    all_to_all x2, waiting for transfers between devices, to_split(): lax.all_to_all(stacks, 'orb', split_axis=2, concat_axis=0, tiled=True)  498 us
    all_gather x1, blocking collectives, on_device(): lax.all_gather(density, 'orb', axis=1, tiled=True)  194 us
    all_to_all x2, waiting for transfers between devices, to_whole(): lax.all_to_all(stacks, 'orb', split_axis=0, concat_axis=2, tiled=True)  176 us
    dot_general x28, matrix products, contract(): return jnp.einsum(form, first, second, precision=lax.Precision.HIGHEST)  170 us
    all_gather x3, waiting for transfers between devices, modes_substep(): collision = jnp.sum(lax.all_gather(partial_value, ('mode', 'orb')), axis=0)  116 us
    all_to_all x1, blocking collectives, propagate(): lax.all_to_all(mixed[:, None, :], 'mode', split_axis=0, concat_axis=1, ti...  97.8 us
    all_to_all x1, waiting for transfers between devices, propagate(): lax.all_to_all(flat, 'mode', split_axis=1, concat_axis=0, tiled=True)  94 us
  transfers between devices with their start and end apart: 9, of which 5 were waited for; matrix products, arithmetic and copies ran while one was open for 10% of the time, Pallas kernels for 0%

profile of v1, /device:TPU:0, one launch (start us, length us, event | category | flops | bytes accessed | tf_op | source)
XLA Modules:
  0.0 1594.7 jit_solution(8836876320927381221)
XLA Ops:
  14.6 194.0 %all_gather.28 = f32[2,256,256]{2,1,0:T(8,128)S(1)} all-gather(f32[2,64,256]{2,1,0:T(8,128)S(1)} %copy-done.11), channel_id=1, replica_groups=mesh['mode'=8,'orb'=4] {'orb'}, dimensions={1}, use_global_device_ids=true | all-gather | bytes 655360 | tf_op jit(solution)/shard_map/all_gather | solution.py:69
  208.6 15.9 all_gather.27
  254.6 14.8 add_bitcast_fusion.5
  283.2 7.8 fusion.10
  291.9 115.6 %all-gather.10.cloned.1.call-done = f32[64,256,256]{2,1,0:T(8,128)} async-done(((f32[2,256,256]{2,1,0:T(8,128)}), f32[64,256,256]{2,1,0:T(8,128)}) %all-gather.10.cloned.1.call-update) | async-done | bytes 16777232 | tf_op jit(solution)/shard_map/all_gather | solution.py:43
  473.1 8.3 copy.81
  487.6 12.8 fusion.8
  501.3 245.2 %all-to-all-done.1 = f32[16,2,256,256]{3,0,1,2:T(8,128)} async-done(((f32[16,2,256,256]{3,0,1,2:T(8,128)}), f32[16,2,256,256]{3,0,1,2:T(8,128)}, u32[]{:S(2)}, u32[]{:S(2)}) %all-to-all-start.1) | async-done | bytes 8388640 | tf_op jit(solution)/shard_map/all_to_all | solution.py:53
  746.5 12.2 copy.145
  758.7 9.6 reshape.18
  768.4 11.6 copy.83
  785.0 94.0 %all-to-all-done.2 = f32[64,8,4096]{2,0,1:T(8,128)} async-done(((f32[64,8,4096]{2,0,1:T(8,128)}), f32[64,8,4096]{2,0,1:T(8,128)}, u32[]{:S(2)}, u32[]{:S(2)}) %all-to-all-start.2) | async-done | bytes 8388640 | tf_op jit(solution)/shard_map/all_to_all | solution.py:60
  879.0 29.9 %convolution_bitcast_fusion = f32[512,1,4096]{0,2,1:T(8,128)} fusion(f32[512,4096]{1,0:T(8,128)} %bitcast.42, f32[512,512]{1,0:T(8,128)} %all-gather.8.cloned.1.call-done), kind=kOutput, calls=%fused_computation.19 | convolution fusion | flops 12884901888 | bytes 17825792 | tf_op jit(solution)/shard_map/mn,nx->mx/dot_general | solution.py:11
  908.9 19.3 %copy.84 = f32[512,1,4096]{2,1,0:T(1,128)} copy(f32[512,1,4096]{0,2,1:T(8,128)} %convolution_bitcast_fusion) | data formatting | bytes 16777216 | tf_op jit(solution)/shard_map/broadcast_in_dim | solution.py:63
  928.2 97.8 %all_to_all.99 = f32[512,1,4096]{2,1,0:T(1,128)S(1)} all-to-all(f32[512,1,4096]{2,1,0:T(1,128)} %copy.84), channel_id=1, replica_groups=mesh['mode'=8,'orb'=4] {'mode'}, dimensions={0} | all-to-all | bytes 16777216 | tf_op jit(solution)/shard_map/all_to_all | solution.py:63
  1025.9 8.1 copy.134
  1034.0 8.4 copy.85
  1042.5 9.3 reshape.19
  1057.5 7.0 reduce_sum.28
  1064.6 175.6 %all-to-all-done.4 = f32[64,2,64,256]{3,2,1,0:T(8,128)} async-done(((f32[64,2,64,256]{3,2,1,0:T(8,128)}), f32[64,2,64,256]{3,2,1,0:T(8,128)}, u32[]{:S(2)}, u32[]{:S(2)}) %all-to-all-start.4) | async-done | bytes 8388640 | tf_op jit(solution)/shard_map/all_to_all | solution.py:49
  1288.7 8.0 fusion.6
  1297.6 11.5 copy.95
  1314.7 253.0 %all-to-all-done.5 = f32[16,2,256,256]{3,0,1,2:T(8,128)} async-done(((f32[16,2,256,256]{3,0,1,2:T(8,128)}), f32[16,2,256,256]{3,0,1,2:T(8,128)}, u32[]{:S(2)}, u32[]{:S(2)}) %all-to-all-start.5) | async-done | bytes 8388640 | tf_op jit(solution)/shard_map/all_to_all | solution.py:53
  1567.7 11.6 copy.96
  (99 shorter events, 197.2 us)
Async XLA Ops:
  8.0 6.5 copy-start.13
  8.0 6.6 copy-start.11
  8.0 200.6 %copy-start.12 = (f32[2,64,256]{2,1,0:T(8,128)S(1)}, f32[2,64,256]{2,1,0:T(8,128)}, u32[]{:S(2)}) copy-start(f32[2,64,256]{2,1,0:T(8,128)} %param.7) | copy-start | bytes 393220
  8.0 216.6 %all-to-all-start = ((f32[64,2,64,256]{3,2,1,0:T(8,128)}), f32[64,2,64,256]{3,2,1,0:T(8,128)}, u32[]{:S(2)}, u32[]{:S(2)}) async-start(f32[64,2,64,256]{3,2,1,0:T(8,128)} %param.5), calls=%async_computation | async-start | bytes 16777216 | tf_op jit(solution)/shard_map/all_to_all | solution.py:49
  14.5 392.9 %all-gather.10.cloned.1.call-start = ((), (), s32[]{:S(2)}) async-start(), calls=%async_computation.7 | async-start | bytes 17301504 | tf_op jit(solution)/shard_map/all_gather | solution.py:43
  208.6 205.8 %copy-start.7 = (f32[2,256,256]{2,1,0:T(8,128)}, f32[2,256,256]{2,1,0:T(8,128)S(1)}, u32[]{:S(2)}) copy-start(f32[2,256,256]{2,1,0:T(8,128)S(1)} %all_gather.28) | copy-start | bytes 1572868
  224.5 189.8 %copy-start.8 = (f32[2,256,256]{2,1,0:T(8,128)}, f32[2,256,256]{2,1,0:T(8,128)S(1)}, u32[]{:S(2)}) copy-start(f32[2,256,256]{2,1,0:T(8,128)S(1)} %all_gather.27) | copy-start | bytes 1572868
  228.7 46.1 %copy-start = (f32[4,16,2,64,256]{4,3,0,1,2:T(8,128)}, f32[4,16,2,64,256]{4,3,0,1,2:T(8,128)S(1)}, u32[]{:S(2)}) copy-start(f32[4,16,2,64,256]{4,3,0,1,2:T(8,128)S(1)} %copy.64) | copy-start | bytes 25165828
  274.9 4.9 copy-start.4
  415.3 11.1 slice-start.2
  415.3 11.1 slice-start.3
  449.0 5.4 copy-start.6
  449.0 14.1 slice-start
  454.5 8.6 slice-start.1
  458.8 4.3 copy-start.5
  481.3 265.2 %all-to-all-start.1 = ((f32[16,2,256,256]{3,0,1,2:T(8,128)}), f32[16,2,256,256]{3,0,1,2:T(8,128)}, u32[]{:S(2)}, u32[]{:S(2)}) async-start(f32[16,2,256,256]{3,0,1,2:T(8,128)} %copy.81), calls=%async_computation.1 | async-start | bytes 16777216 | tf_op jit(solution)/shard_map/all_to_all | solution.py:53
  487.0 298.0 %all-gather.8.cloned.1.call-start = ((), (), s32[]{:S(2)}) async-start(), calls=%async_computation.6 | async-start | bytes 1179648 | tf_op jit(solution)/shard_map/all_gather | solution.py:62
  487.6 569.9 %all-gather.12.cloned.1.call-start = ((), (), s32[]{:S(2)}) async-start(), calls=%async_computation.8 | async-start | bytes 17301504 | tf_op jit(solution)/shard_map/all_gather | solution.py:43
  780.0 99.0 %all-to-all-start.2 = ((f32[64,8,4096]{2,0,1:T(8,128)}), f32[64,8,4096]{2,0,1:T(8,128)}, u32[]{:S(2)}, u32[]{:S(2)}) async-start(f32[64,8,4096]{2,0,1:T(8,128)} %copy.83), calls=%async_computation.2 | async-start | bytes 16777216 | tf_op jit(solution)/shard_map/all_to_all | solution.py:60
  1051.7 188.5 %all-to-all-start.4 = ((f32[64,2,64,256]{3,2,1,0:T(8,128)}), f32[64,2,64,256]{3,2,1,0:T(8,128)}, u32[]{:S(2)}, u32[]{:S(2)}) async-start(f32[64,2,64,256]{3,2,1,0:T(8,128)} %reshape.19), calls=%async_computation.4 | async-start | bytes 16777216 | tf_op jit(solution)/shard_map/all_to_all | solution.py:49
  1057.4 521.9 %all-gather.14.cloned.1.call-start = ((), (), s32[]{:S(2)}) async-start(), calls=%async_computation.9 | async-start | bytes 17301504 | tf_op jit(solution)/shard_map/all_gather | solution.py:43
  1057.5 7.0 copy-start.9
  1057.5 7.0 copy-start.10
  1309.1 258.7 %all-to-all-start.5 = ((f32[16,2,256,256]{3,0,1,2:T(8,128)}), f32[16,2,256,256]{3,0,1,2:T(8,128)}, u32[]{:S(2)}, u32[]{:S(2)}) async-start(f32[16,2,256,256]{3,0,1,2:T(8,128)} %copy.95), calls=%async_computation.5 | async-start | bytes 16777216 | tf_op jit(solution)/shard_map/all_to_all | solution.py:53
  (3 other events, 10.1 us)
Sparse Core Ops, SparseCore 0:
  292.0 115.4 all-gather.9
  1297.7 269.0 all-gather.13
Sparse Core Ops, SparseCore 1:
  489.4 23.6 all-gather.7
  515.9 236.7 all-gather.11
